TPU v7x, 32 devices: a whole 2x2x4 slice. The times are simulated.
32 devices in a mesh: groups: 2 (over x), span: 16 (over z, y, core).
Axes of the slice: x: 2, y: 2, z: 4, core: 2. Of those that a mesh axis runs over, the one named last changes fastest.
Arguments:
- queries: bfloat16 [8192, 1024], P(('groups', 'span')), parts along dimension 0, may hold values from -96 to 96
- keys: bfloat16 [8192, 1024], P(('groups', 'span')), parts along dimension 0, may hold values from -9 to 9
- values: bfloat16 [8192, 1024], P(('groups', 'span')), parts along dimension 0, may hold values from -6 to 6
- track: int32 [64, 16], P(('groups', 'span')), parts along dimension 0, may hold values 0 or 1
- out_weight: bfloat16 [1024, 1024], replicated, may hold values from -0.1875 to 0.1875
- grad_out: bfloat16 [8192, 1024], P(('groups', 'span')), parts along dimension 0, may hold values from -6 to 6
Outputs:
- query_grad: bfloat16 [8192, 1024], P(('groups', 'span')), parts along dimension 0
- key_grad: bfloat16 [8192, 1024], P(('groups', 'span')), parts along dimension 0
- value_grad: bfloat16 [8192, 1024], P(('groups', 'span')), parts along dimension 0
- weight_grad: float32 [2048, 1024], P(('groups', 'span')), parts along dimension 0
There are 2 independent parts, one for each index of `groups`. A program takes and returns all parts, laid end to end along the dimension named above; an argument that names none is the same for every part. Nothing has to cross between parts.
All inputs are finite; a program needn't handle non-finite values. No bound on the sum of `track` on one device may be relied on, other than what follows from the above.
Results may differ from a plain program's by a relative error of at most 0.039.
Values may be sent and summed in bfloat16 or wider, within the bound.
A program may use at most 64 MiB of HBM per device.

v0:
```python
import jax
import jax.numpy as jnp
from jax import lax
from jax.sharding import PartitionSpec as P

HEADS = 16
BLOCK = 128
WINDOW = 8


def shifted(value, axis, steps):
    count = lax.axis_size(axis)
    initial, last = (max(0, -steps), min(count, count - steps))
    return lax.ppermute(value, axis, [(source, source + steps) for source in range(initial, last)])


def pair_grads(query_p, key_p, value_p, grad_p, allowed, local_count, scale):
    scores = jnp.einsum("rhd,khd->hrk", query_p, key_p, preferred_element_type=jnp.float32) * scale
    scores = jnp.where(allowed[None], scores, jnp.float32(-1e30))
    top = jnp.max(scores, axis=-1, keepdims=True)
    expo = jnp.exp(scores - top)
    probs = expo / jnp.sum(expo, axis=-1, keepdims=True)
    probs_low = probs.astype(jnp.bfloat16)
    attn = jnp.einsum(
        "hrk,khd->rhd", probs_low, value_p, preferred_element_type=jnp.float32
    ).astype(jnp.bfloat16)
    delta = jnp.einsum("rhd,rhd->hr", grad_p, attn, preferred_element_type=jnp.float32)
    dprob = jnp.einsum("rhd,khd->hrk", grad_p, value_p, preferred_element_type=jnp.float32)
    dscore = (probs * (dprob - delta[..., None])).astype(jnp.bfloat16)
    query_g = (
        jnp.einsum("hrk,khd->rhd", dscore, key_p, preferred_element_type=jnp.float32) * scale
    ).astype(jnp.bfloat16)
    key_g = (
        jnp.einsum(
            "hrk,rhd->khd", dscore[:, :, :local_count], query_p, preferred_element_type=jnp.float32
        )
        * scale
    ).astype(jnp.bfloat16)
    value_g = jnp.einsum(
        "hrk,rhd->khd", probs_low[:, :, :local_count], grad_p, preferred_element_type=jnp.float32
    ).astype(jnp.bfloat16)
    return (attn, query_g, key_g, value_g)


def shards(queries, keys, values, track, out_weight, grad_out):
    rows, width = queries.shape
    head_dim = width // HEADS
    pair_width = 2 * head_dim
    scale = head_dim ** (-0.5)
    span_id = lax.axis_index("span")
    stacked = jnp.stack([keys, values])
    received = [shifted(stacked, "span", distance) for distance in range(1, WINDOW + 1)]
    memory = jnp.concatenate(received, axis=1)
    all_keys = jnp.concatenate([keys, memory[0]], axis=0)
    all_values = jnp.concatenate([values, memory[1]], axis=0)
    grad_attn = lax.dot_general(
        grad_out, out_weight, (((1,), (1,)), ((), ())), preferred_element_type=jnp.float32
    ).astype(jnp.bfloat16)
    per_block = rows // BLOCK
    lookback = jnp.arange(WINDOW * per_block, dtype=jnp.int32) // per_block + 1
    block_ok = (track == 1) & (lookback[None, :] <= span_id)
    mem_ok = jnp.repeat(jnp.repeat(block_ok, BLOCK, axis=0), BLOCK, axis=1)
    position = jnp.arange(rows, dtype=jnp.int32)
    local_ok = position[:, None] >= position[None, :]
    allowed = jnp.concatenate([local_ok, mem_ok], axis=1)
    key_total = all_keys.shape[0]

    def head_pair(index, carry):
        attn_buf, query_buf, key_buf, value_buf = carry
        start = index * pair_width
        query_p = lax.dynamic_slice_in_dim(queries, start, pair_width, 1).reshape(rows, 2, head_dim)
        key_p = lax.dynamic_slice_in_dim(all_keys, start, pair_width, 1).reshape(
            key_total, 2, head_dim
        )
        value_p = lax.dynamic_slice_in_dim(all_values, start, pair_width, 1).reshape(
            key_total, 2, head_dim
        )
        grad_p = lax.dynamic_slice_in_dim(grad_attn, start, pair_width, 1).reshape(
            rows, 2, head_dim
        )
        attn, query_g, key_g, value_g = pair_grads(
            query_p, key_p, value_p, grad_p, allowed, rows, scale
        )
        attn_buf = lax.dynamic_update_slice_in_dim(
            attn_buf, attn.reshape(rows, pair_width), start, 1
        )
        query_buf = lax.dynamic_update_slice_in_dim(
            query_buf, query_g.reshape(rows, pair_width), start, 1
        )
        key_buf = lax.dynamic_update_slice_in_dim(
            key_buf, key_g.reshape(rows, pair_width), start, 1
        )
        value_buf = lax.dynamic_update_slice_in_dim(
            value_buf, value_g.reshape(rows, pair_width), start, 1
        )
        return (attn_buf, query_buf, key_buf, value_buf)

    empty = jnp.zeros((rows, width), jnp.bfloat16)
    attn_out, query_grad, key_grad, value_grad = lax.fori_loop(
        0, HEADS // 2, head_pair, (empty, empty, empty, empty)
    )
    weight_grad = lax.psum_scatter(
        lax.dot_general(
            attn_out, grad_out, (((0,), (0,)), ((), ())), preferred_element_type=jnp.float32
        ),
        "span",
        scatter_dimension=0,
        tiled=True,
    )
    return (query_grad, key_grad, value_grad, weight_grad)


def solution(mesh):
    in_specs = (
        P(("groups", "span"), None),
        P(("groups", "span"), None),
        P(("groups", "span"), None),
        P(("groups", "span"), None),
        P(),
        P(("groups", "span"), None),
    )
    out_specs = (
        P(("groups", "span"), None),
        P(("groups", "span"), None),
        P(("groups", "span"), None),
        P(("groups", "span"), None),
    )
    return jax.shard_map(shards, mesh=mesh, in_specs=in_specs, out_specs=out_specs, check_vma=False)
```

profile of v0, /device:TPU:28, one launch (start us, length us, event | category | flops | bytes accessed | tf_op | source)
XLA Modules:
  0.0 513.7 jit_solution(15153567718506939762)
XLA Ops:
  7.2 1.4 copy.12
  10.9 1.9 collective-permute-start
  20.4 15.6 %collective-permute-done = bf16[2,256,1024]{1,2,0:T(8,128)(2,1)} collective-permute-done((bf16[2,256,1024]{1,2,0:T(8,128)(2,1)}, bf16[2,256,1024]{1,2,0:T(8,128)(2,1)}, u32[]{:S(2)}, u32[]{:S(2)}) %collective-permute-start) | collective-permute-done | bytes 1048608 | tf_op jit(solution)/shard_map/ppermute | solution.py:14
  38.2 3.0 collective-permute-done.1
  42.4 38.5 %collective-permute-done.2 = bf16[2,256,1024]{1,2,0:T(8,128)(2,1)} collective-permute-done((bf16[2,256,1024]{1,2,0:T(8,128)(2,1)}, bf16[2,256,1024]{1,2,0:T(8,128)(2,1)}, u32[]{:S(2)}, u32[]{:S(2)}) %collective-permute-start.2) | collective-permute-done | bytes 1048608 | tf_op jit(solution)/shard_map/ppermute | solution.py:14
  82.2 2.6 convolution_convert_fusion.2
  86.2 1.4 constant_dynamic-update-slice_fusion.10
  87.5 1.4 constant_dynamic-update-slice_fusion.9
  88.9 1.4 constant_dynamic-update-slice_fusion.8
  90.3 1.4 constant_dynamic-update-slice_fusion.7
  93.7 155.7 %collective-permute-done.6 = bf16[2,256,1024]{1,2,0:T(8,128)(2,1)} collective-permute-done((bf16[2,256,1024]{1,2,0:T(8,128)(2,1)}, bf16[2,256,1024]{1,2,0:T(8,128)(2,1)}, u32[]{:S(2)}, u32[]{:S(2)}) %collective-permute-start.6) | collective-permute-done | bytes 1048608 | tf_op jit(solution)/shard_map/ppermute | solution.py:14
  250.7 3.8 collective-permute-done.7
  257.0 4.0 pad_maximum_fusion
  264.4 159.1 %while.19 = (s32[]{:T(128)}, bf16[256,1024]{0,1:T(8,128)(2,1)}, bf16[256,1024]{1,0:T(8,128)(2,1)}, bf16[256,1024]{1,0:T(8,128)(2,1)}, bf16[256,1024]{1,0:T(8,128...) while((s32[]{:T(128)}, bf16[256,1024]{0,1:T(8,128)(2,1)}, ...), condition=%wide.region_3.4_spmd, body=%wide.region_0.3_spmd.sunk | while | flops 649660160 | bytes 69216552 | solution.py:99
  268.6 5.0 fusion.63
  273.6 3.0 fusion.64
  288.5 5.0 fusion.63
  293.5 3.0 fusion.64
  308.4 5.0 fusion.63
  313.3 3.0 fusion.64
  328.2 5.0 fusion.63
  333.2 3.0 fusion.64
  348.1 5.0 fusion.63
  353.1 3.0 fusion.64
  368.0 5.0 fusion.63
  373.0 3.0 fusion.64
  387.9 5.0 fusion.63
  392.9 3.0 fusion.64
  407.8 5.0 fusion.63
  412.8 3.0 fusion.64
  423.5 3.9 fusion.18
  427.4 79.5 %reduce-scatter.2.cloned.1.call-done = f32[64,1024]{1,0:T(8,128)} async-done(((f32[1024,1024]{1,0:T(8,128)}), f32[64,1024]{1,0:T(8,128)}) %reduce-scatter.2.cloned.1.call-update) | async-done | bytes 262160 | tf_op jit(solution)/shard_map/reduce_scatter | solution.py:102
  (216 shorter events, 119.8 us)
Async XLA Ops:
  7.2 75.0 %copy-start = (bf16[1024,1024]{1,0:T(8,128)(2,1)S(1)}, bf16[1024,1024]{1,0:T(8,128)(2,1)}, u32[]{:S(2)}) copy-start(bf16[1024,1024]{1,0:T(8,128)(2,1)} %param.12) | copy-start | bytes 6291460
  7.2 499.7 %reduce-scatter.2.cloned.1.call-start = ((), (), s32[]{:S(2)}) async-start(), calls=%async_computation.1 | async-start | bytes 4456448 | tf_op jit(solution)/shard_map/reduce_scatter | solution.py:102
  10.9 25.1 %collective-permute-start = (bf16[2,256,1024]{1,2,0:T(8,128)(2,1)}, bf16[2,256,1024]{1,2,0:T(8,128)(2,1)}, u32[]{:S(2)}, u32[]{:S(2)}) collective-permute-start(bf16[2,256,1024]{1,2,0:T(8,128)(2,1)} %pad_maximum_fusion.2), channel_id=1, source_target_pairs={{0,1},{1,2},{2,3},{3,4},{4,5},{5,6},{6,7},{7,8},{8,9},{9,10},{10,1... | collective-permute-start | bytes 3145736 | tf_op jit(solution)/shard_map/ppermute | solution.py:14
  12.8 28.3 %collective-permute-start.1 = (bf16[2,256,1024]{1,2,0:T(8,128)(2,1)}, bf16[2,256,1024]{1,2,0:T(8,128)(2,1)}, u32[]{:S(2)}, u32[]{:S(2)}) collective-permute-start(bf16[2,256,1024]{1,2,0:T(8,128)(2,1)} %pad_maximum_fusion.2), channel_id=1, source_target_pairs={{0,2},{1,3},{2,4},{3,5},{4,6},{5,7},{6,8},{7,9},{8,10},{9,11},{10,... | collective-permute-start | bytes 3145736 | tf_op jit(solution)/shard_map/ppermute | solution.py:14
  14.1 66.8 %collective-permute-start.2 = (bf16[2,256,1024]{1,2,0:T(8,128)(2,1)}, bf16[2,256,1024]{1,2,0:T(8,128)(2,1)}, u32[]{:S(2)}, u32[]{:S(2)}) collective-permute-start(bf16[2,256,1024]{1,2,0:T(8,128)(2,1)} %pad_maximum_fusion.2), channel_id=1, source_target_pairs={{0,3},{1,4},{2,5},{3,6},{4,7},{5,8},{6,9},{7,10},{8,11},{9,12},{10... | collective-permute-start | bytes 3145736 | tf_op jit(solution)/shard_map/ppermute | solution.py:14
  15.4 73.5 %collective-permute-start.3 = (bf16[2,256,1024]{1,2,0:T(8,128)(2,1)}, bf16[2,256,1024]{1,2,0:T(8,128)(2,1)}, u32[]{:S(2)}, u32[]{:S(2)}) collective-permute-start(bf16[2,256,1024]{1,2,0:T(8,128)(2,1)} %pad_maximum_fusion.2), channel_id=1, source_target_pairs={{0,4},{1,5},{2,6},{3,7},{4,8},{5,9},{6,10},{7,11},{8,12},{9,13},{1... | collective-permute-start | bytes 3145736 | tf_op jit(solution)/shard_map/ppermute | solution.py:14
  16.7 73.5 %collective-permute-start.4 = (bf16[2,256,1024]{1,2,0:T(8,128)(2,1)}, bf16[2,256,1024]{1,2,0:T(8,128)(2,1)}, u32[]{:S(2)}, u32[]{:S(2)}) collective-permute-start(bf16[2,256,1024]{1,2,0:T(8,128)(2,1)} %pad_maximum_fusion.2), channel_id=1, source_target_pairs={{0,5},{1,6},{2,7},{3,8},{4,9},{5,10},{6,11},{7,12},{8,13},{9,14},{... | collective-permute-start | bytes 3145736 | tf_op jit(solution)/shard_map/ppermute | solution.py:14
  36.0 56.3 %collective-permute-start.5 = (bf16[2,256,1024]{1,2,0:T(8,128)(2,1)}, bf16[2,256,1024]{1,2,0:T(8,128)(2,1)}, u32[]{:S(2)}, u32[]{:S(2)}) collective-permute-start(bf16[2,256,1024]{1,2,0:T(8,128)(2,1)} %pad_maximum_fusion.2), channel_id=1, source_target_pairs={{0,6},{1,7},{2,8},{3,9},{4,10},{5,11},{6,12},{7,13},{8,14},{9,15},... | collective-permute-start | bytes 3145736 | tf_op jit(solution)/shard_map/ppermute | solution.py:14
  41.1 208.2 %collective-permute-start.6 = (bf16[2,256,1024]{1,2,0:T(8,128)(2,1)}, bf16[2,256,1024]{1,2,0:T(8,128)(2,1)}, u32[]{:S(2)}, u32[]{:S(2)}) collective-permute-start(bf16[2,256,1024]{1,2,0:T(8,128)(2,1)} %pad_maximum_fusion.2), channel_id=1, source_target_pairs={{0,7},{1,8},{2,9},{3,10},{4,11},{5,12},{6,13},{7,14},{8,15},{16,23... | collective-permute-start | bytes 3145736 | tf_op jit(solution)/shard_map/ppermute | solution.py:14
  80.9 173.6 %collective-permute-start.7 = (bf16[2,256,1024]{1,2,0:T(8,128)(2,1)}, bf16[2,256,1024]{1,2,0:T(8,128)(2,1)}, u32[]{:S(2)}, u32[]{:S(2)}) collective-permute-start(bf16[2,256,1024]{1,2,0:T(8,128)(2,1)} %pad_maximum_fusion.2), channel_id=1, source_target_pairs={{0,8},{1,9},{2,10},{3,11},{4,12},{5,13},{6,14},{7,15},{16,24},{17,... | collective-permute-start | bytes 3145736 | tf_op jit(solution)/shard_map/ppermute | solution.py:14
  273.6 4.5 copy-start.2
  276.6 2.4 copy-start.1
  279.0 1.4 copy-start.3
  293.5 4.5 copy-start.2
  296.5 2.4 copy-start.1
  298.9 1.4 copy-start.3
  313.3 4.5 copy-start.2
  316.4 2.4 copy-start.1
  318.8 1.4 copy-start.3
  333.2 4.5 copy-start.2
  336.2 2.4 copy-start.1
  338.7 1.4 copy-start.3
  353.1 4.5 copy-start.2
  356.1 2.4 copy-start.1
  358.5 1.4 copy-start.3
  373.0 4.5 copy-start.2
  376.0 2.4 copy-start.1
  378.4 1.4 copy-start.3
  392.9 4.5 copy-start.2
  395.9 2.4 copy-start.1
  412.8 4.5 copy-start.2
  415.8 2.4 copy-start.1
  (2 other events, 2.8 us)
Sparse Core Ops, SparseCore 0:
  427.5 79.2 reduce-scatter.1
where the time goes:
time: 521 us; the launch traced here: 514 us
  waiting for transfers between devices  297 us (57%)
  matrix products  85 us (16%)
  local copies, waits for them, and re-layouts  75.6 us (15%)
  other arithmetic  30.6 us (6%)
  between operations  14.2 us (3%)
  starting transfers between devices  11 us (2%)
    ppermute x8, waiting for transfers between devices, shifted(): lax.ppermute(value, axis, [(source, source + steps) for source in range(i...  217 us
    reduce_scatter x1, waiting for transfers between devices, shards(): lax.psum_scatter(lax.dot_general(attn_out, grad_out, (((0,), (0,)), ((),...  79.5 us
    sub x8, matrix products, pair_grads(): expo = jnp.exp(scores - top)  39.9 us
    convert_element_type x8, other arithmetic, pair_grads(): probs_low = probs.astype(jnp.bfloat16)  24 us
    unnamed x12, local copies, waits for them, and re-layouts  12.5 us
    ppermute x8, starting transfers between devices, shifted(): lax.ppermute(value, axis, [(source, source + steps) for source in range(i...  10.9 us
  transfers between devices with their start and end apart: 9, of which 7 were waited for; matrix products, arithmetic and copies ran while one was open for 3% of the time, Pallas kernels for 0%

commit v1 on v0

v1 whole, which is shorter than its diff:
```python
import functools

import jax
import jax.numpy as jnp
from jax import lax
from jax.experimental import pallas as pl
from jax.experimental.pallas import tpu as pltpu
from jax.sharding import PartitionSpec as P

HEADS = 16
BLOCK = 128
PLANE = 4
OWN = 8
SLOTS = 9
PAIR = 128
F32 = jnp.float32
BF16 = jnp.bfloat16
MESH = pl.DeviceIdType.MESH
NT = (((1,), (1,)), ((), ()))


def dot(a, b):
    return jnp.dot(a, b, preferred_element_type=F32)


def kernel(
    n, chunks, k_hbm, v_hbm, q_ref, w_ref, go_ref, bias_ref,
    dq_ref, dk_ref, dv_ref, wg_ref,
    kv, kt, vt, s_scr, own_sem, send_sem, recv_sem,
):
    rows = q_ref.shape[0]
    head_dim = PAIR // 2
    scale = head_dim ** (-0.5)
    sid = lax.axis_index("span")
    gid = lax.axis_index("groups")
    i = lax.rem(sid, PLANE)
    z = sid // PLANE
    y = i // 2
    c = lax.rem(i, 2)
    nz = n // PLANE
    yp = sid + 2 - 4 * y
    cp = sid + 1 - 2 * c
    iy = i + 2 - 4 * y
    ic = i + 1 - 2 * c
    iyc = iy + 1 - 2 * c
    up = lax.rem(sid + PLANE, n)
    down = lax.rem(sid + n - PLANE, n)
    has_up = z < nz - 1
    has1 = z >= 1
    has2 = z >= 2

    def own_copy(ch, which):
        src = k_hbm if which == 0 else v_hbm
        cols = pl.ds(pl.multiple_of(ch * PAIR, PAIR), PAIR)
        return pltpu.make_async_copy(src.at[:, cols], kv.at[ch, OWN, which], own_sem.at[ch, which])

    for ch in range(chunks):
        for which in range(2):
            own_copy(ch, which).start()

    def copy(ch, src_slot, dst_slot, target, kind):
        return pltpu.make_async_remote_copy(
            src_ref=kv.at[ch, src_slot],
            dst_ref=kv.at[ch, dst_slot],
            send_sem=send_sem.at[kind, ch],
            recv_sem=recv_sem.at[ch, dst_slot],
            device_id=(gid, target),
            device_id_type=MESH,
        )

    def arrived(ch, slot):
        copy(ch, slot, slot, cp, 0).wait_recv()

    @pl.when(jnp.logical_not(has1))
    def _():
        kv[:, 0:4] = jnp.zeros((chunks, 4, 2, rows, PAIR), BF16)

    for j in range(PLANE):
        @pl.when(jnp.logical_and(jnp.logical_not(has2), i <= j))
        def _():
            kv[:, 4 + j] = jnp.zeros((chunks, 2, rows, PAIR), BF16)

    barrier = pltpu.get_barrier_semaphore()
    for neighbour in (yp, cp):
        pl.semaphore_signal(barrier, inc=1, device_id=(gid, neighbour), device_id_type=MESH)

    @pl.when(has_up)
    def _():
        pl.semaphore_signal(barrier, inc=1, device_id=(gid, up), device_id_type=MESH)

    @pl.when(has1)
    def _():
        pl.semaphore_signal(barrier, inc=1, device_id=(gid, down), device_id_type=MESH)

    pl.semaphore_wait(barrier, 2 + (2 * nz - 2 - z) // nz + (z + nz - 1) // nz)

    relay_z = jnp.logical_and(has1, has_up)
    y1, y0 = y == 1, y == 0
    c1, c0 = c == 1, c == 0

    def stage0(ch):
        own_copy(ch, 0).wait()
        own_copy(ch, 1).wait()

        @pl.when(has_up)
        def _():
            copy(ch, OWN, i, up, 0).start()

        @pl.when(y0)
        def _():
            copy(ch, OWN, 4 + i, yp, 5).start()

        @pl.when(c0)
        def _():
            copy(ch, OWN, 4 + i, cp, 6).start()

    def stage1(ch):
        @pl.when(has1)
        def _():
            arrived(ch, i)

            @pl.when(has_up)
            def _():
                copy(ch, i, 4 + i, up, 1).start()

            copy(ch, i, i, yp, 2).start()
            copy(ch, i, i, cp, 3).start()

        @pl.when(y1)
        def _():
            arrived(ch, 4 + iy)
            copy(ch, 4 + iy, 4 + iy, cp, 7).start()

    def stage2(ch):
        @pl.when(has2)
        def _():
            arrived(ch, 4 + i)

            @pl.when(y1)
            def _():
                copy(ch, 4 + i, 4 + i, yp, 5).start()

            @pl.when(c1)
            def _():
                copy(ch, 4 + i, 4 + i, cp, 6).start()

        @pl.when(has1)
        def _():
            arrived(ch, iy)
            copy(ch, iy, iy, cp, 4).start()

    def stage3(ch):
        @pl.when(jnp.logical_and(y0, has2))
        def _():
            arrived(ch, 4 + iy)
            copy(ch, 4 + iy, 4 + iy, cp, 7).start()

    def stage4(ch):
        @pl.when(has1)
        def _():
            arrived(ch, ic)
            arrived(ch, iyc)

        @pl.when(jnp.logical_or(c1, has2))
        def _():
            arrived(ch, 4 + ic)

        @pl.when(jnp.logical_or(y1, has2))
        def _():
            arrived(ch, 4 + iyc)

    def sent(ch):
        def done(kind):
            copy(ch, OWN, OWN, cp, kind).wait_send()

        @pl.when(has_up)
        def _():
            done(0)

        @pl.when(relay_z)
        def _():
            done(1)

        @pl.when(has1)
        def _():
            done(2)
            done(3)
            done(4)

        @pl.when(jnp.logical_or(y0, has2))
        def _():
            done(5)

        @pl.when(jnp.logical_or(c0, has2))
        def _():
            done(6)

        @pl.when(jnp.logical_or(y1, has2))
        def _():
            done(7)

    def compute(ch):
        cols = pl.ds(pl.multiple_of(ch * PAIR, PAIR), PAIR)
        go = go_ref[...]
        q32 = q_ref[:, cols].astype(F32) * scale
        qs = q32.astype(BF16)
        q_t = q32.T.astype(BF16)
        g_t = lax.dot_general(w_ref[cols, :], go, NT, preferred_element_type=F32).astype(BF16)
        g32_t = g_t.astype(F32)
        g = g32_t.T.astype(BF16)
        head_row = lax.broadcasted_iota(jnp.int32, (PAIR, rows), 0) // head_dim
        head_col = lax.broadcasted_iota(jnp.int32, (rows, PAIR), 1) // head_dim
        causal = lax.broadcasted_iota(jnp.int32, (rows, rows), 0) <= lax.broadcasted_iota(
            jnp.int32, (rows, rows), 1
        )
        for b in range(SLOTS):
            kt[b] = kv[ch, b, 0].T
            vt[b] = kv[ch, b, 1].T
        dk = jnp.zeros((rows, PAIR), F32)
        dv = jnp.zeros((rows, PAIR), F32)
        attn_parts = []
        dq_parts = []
        zero = jnp.zeros((), BF16)
        for h in range(2):
            span = pl.ds(h * head_dim, head_dim)
            q_th = jnp.where(head_row == h, q_t, zero)
            g_th = jnp.where(head_row == h, g_t, zero)
            top = None
            for b in range(SLOTS):
                s = dot(kv[ch, b, 0], q_th)
                if b == OWN:
                    s = jnp.where(causal, s, F32(-1e30))
                else:
                    s = jnp.concatenate(
                        [
                            s[:BLOCK] + bias_ref[2 * b : 2 * b + 1, :],
                            s[BLOCK:] + bias_ref[2 * b + 1 : 2 * b + 2, :],
                        ],
                        axis=0,
                    )
                s_scr[b] = s
                peak = jnp.max(s, axis=0, keepdims=True)
                top = peak if top is None else jnp.maximum(top, peak)
            total = jnp.zeros((1, rows), F32)
            attn = jnp.zeros((head_dim, rows), F32)
            for b in range(SLOTS):
                e = jnp.exp(s_scr[b] - top)
                s_scr[b] = e
                total = total + jnp.sum(e, axis=0, keepdims=True)
                attn = attn + dot(vt[b, span, :], e.astype(BF16))
            inv = 1.0 / total
            attn_low = (attn * inv).astype(BF16)
            delta = jnp.sum(
                g32_t[h * head_dim : (h + 1) * head_dim] * attn_low.astype(F32),
                axis=0,
                keepdims=True,
            )
            dq = jnp.zeros((head_dim, rows), F32)
            for b in range(SLOTS):
                e = s_scr[b]
                ds = e * (dot(kv[ch, b, 1], g_th) - delta)
                dq = dq + dot(kt[b, span, :], ds.astype(BF16))
                if b == OWN:
                    dk = dk + dot(
                        (ds * inv).astype(BF16), jnp.where(head_col == h, qs, zero)
                    )
                    dv = dv + dot((e * inv).astype(BF16), jnp.where(head_col == h, g, zero))
            attn_parts.append(attn_low)
            dq_parts.append(dq * (inv * scale))
        dq_ref[:, cols] = jnp.concatenate(dq_parts, axis=0).T.astype(BF16)
        dk_ref[:, cols] = dk.astype(BF16)
        dv_ref[:, cols] = dv.astype(BF16)
        wg_ref[cols, :] = dot(jnp.concatenate(attn_parts, axis=0), go)

    def step(t, carry):
        for lag, stage in enumerate((stage0, stage1, stage2, stage3)):
            @pl.when(jnp.logical_and(t >= lag, t < chunks + lag))
            def _():
                stage(t - lag)

        @pl.when(t >= 4)
        def _():
            stage4(t - 4)
            compute(t - 4)

        return carry

    lax.fori_loop(0, chunks + 4, step, 0)

    def finish(ch, carry):
        sent(ch)
        return carry

    lax.fori_loop(0, chunks, finish, 0)


def block_bias(track, sid, rows):
    i = lax.rem(sid, PLANE)
    slot = jnp.arange(2 * OWN, dtype=jnp.int32) // 2
    half = jnp.arange(2 * OWN, dtype=jnp.int32) % 2
    gap = i - lax.rem(slot, PLANE)
    look = jnp.where(slot < PLANE, gap + 4, jnp.where(gap > 0, gap, gap + 8))
    column = (look - 1) * 2 + half
    pick = column[:, None] == jnp.arange(track.shape[1], dtype=jnp.int32)[None, :]
    chosen = jnp.sum(jnp.where(pick[None], track[:, None, :], 0), axis=-1)
    ok = (chosen == 1) & (look <= sid)[None, :]
    return jnp.repeat(jnp.where(ok, 0.0, -1e30).astype(F32).T, BLOCK, axis=1)


def shards(n, queries, keys, values, track, out_weight, grad_out):
    rows, width = queries.shape
    chunks = width // PAIR
    sid = lax.axis_index("span")
    bias = block_bias(track, sid, rows)
    grad = jax.ShapeDtypeStruct((rows, width), BF16)
    vmem = pl.BlockSpec(memory_space=pltpu.VMEM)
    dq, dk, dv, wg = pl.pallas_call(
        functools.partial(kernel, n, chunks),
        out_shape=(grad, grad, grad, jax.ShapeDtypeStruct((width, width), F32)),
        in_specs=[pl.BlockSpec(memory_space=pl.ANY)] * 2 + [vmem] * 4,
        out_specs=(vmem,) * 4,
        scratch_shapes=[
            pltpu.VMEM((chunks, SLOTS, 2, rows, PAIR), BF16),
            pltpu.VMEM((SLOTS, PAIR, rows), BF16),
            pltpu.VMEM((SLOTS, PAIR, rows), BF16),
            pltpu.VMEM((SLOTS, rows, rows), F32),
            pltpu.SemaphoreType.DMA((chunks, 2)),
            pltpu.SemaphoreType.DMA((8, chunks)),
            pltpu.SemaphoreType.DMA((chunks, OWN)),
        ],
        compiler_params=pltpu.CompilerParams(
            collective_id=0, has_side_effects=True, vmem_limit_bytes=60 * 1024 * 1024
        ),
    )(keys, values, queries, out_weight, grad_out, bias)
    weight_grad = lax.psum_scatter(wg, "span", scatter_dimension=0, tiled=True)
    return (dq, dk, dv, weight_grad)


def solution(mesh):
    split = P(("groups", "span"), None)
    return jax.shard_map(
        functools.partial(shards, mesh.shape["span"]),
        mesh=mesh,
        in_specs=(split, split, split, split, P(), split),
        out_specs=(split,) * 4,
        check_vma=False,
    )
```

time: 521 us -> 164 us (0.31)
  the two profiles are of different devices: /device:TPU:28 before, /device:TPU:0 now
where the time goes in v1:
time: 164 us
  waiting for transfers between devices  98.5 us (60%)
  Pallas kernels  47.5 us (29%)
  between operations  14.1 us (9%)
  local copies, waits for them, and re-layouts  3.18 us (2%)
    reduce_scatter x1, waiting for transfers between devices, shards(): weight_grad = lax.psum_scatter(wg, 'span', scatter_dimension=0, tiled=True)  98.5 us
    pallas_call x1, Pallas kernels, shards(): pl.pallas_call(functools.partial(kernel, n, chunks), out_shape=(grad, gra...  47.5 us
  transfers between devices with their start and end apart: 1, of which 1 were waited for; matrix products, arithmetic and copies ran while one was open for 0% of the time, Pallas kernels for 0%

profile of v1, /device:TPU:0, one launch (start us, length us, event | category | flops | bytes accessed | tf_op | source)
XLA Modules:
  0.0 164.2 jit_solution(5052752484082136497)
XLA Ops:
  7.2 0.0 reduce-scatter.2.cloned.1.call-start
  7.2 0.1 iota_compare_fusion
  7.3 0.8 select_reduce_fusion
  8.1 0.1 copy.10
  8.2 0.1 broadcast_in_dim.41
  8.3 0.6 copy.13
  8.9 47.5 %shard_map.93 = (bf16[256,1024]{1,0:T(8,128)(2,1)}, bf16[256,1024]{1,0:T(8,128)(2,1)}, bf16[256,1024]{1,0:T(8,128)(2,1)}, f32[1024,1024]{1,0:T(8,128)}) custom-call(bf16[256,1024]{1,0:T(8,128)(2,1)} %k_hbm.1, bf16[256,1024]{1,0:T(8,128)(2,1)} %v_hbm.1, bf16[256,1024]{1,0:T(8,128)(2,1)} %q_ref.1, bf16[1024,1024]{1,0:T(8,128)(2,1)} %w_ref.1, ...), custom_call_target="tpu_custom_call" | custom-call | tf_op jit(solution)/shard_map/pallas_call | solution.py:317
  56.4 0.0 copy-start.2
  56.4 0.0 copy-start.1
  56.4 0.0 copy-start
  56.4 0.0 reduce-scatter.2.cloned.1.call-update
  56.4 98.5 %reduce-scatter.2.cloned.1.call-done = f32[64,1024]{1,0:T(8,128)} async-done(((f32[1024,1024]{1,0:T(8,128)}), f32[64,1024]{1,0:T(8,128)}) %reduce-scatter.2.cloned.1.call-update) | async-done | bytes 262160 | tf_op jit(solution)/shard_map/reduce_scatter | solution.py:335
  155.0 0.0 copy-done.2
  155.0 0.8 copy.17
  155.8 0.0 copy-done.1
  155.8 0.8 copy.18
  156.6 0.0 copy-done
  156.6 0.8 copy.19
  (3 shorter events, 0.0 us)
Async XLA Ops:
  7.2 147.8 %reduce-scatter.2.cloned.1.call-start = ((), (), s32[]{:S(2)}) async-start(), calls=%async_computation.1 | async-start | bytes 4456448 | tf_op jit(solution)/shard_map/reduce_scatter | solution.py:335
  56.4 98.6 %copy-start.2 = (bf16[256,1024]{1,0:T(8,128)(2,1)S(1)}, bf16[256,1024]{1,0:T(8,128)(2,1)}, u32[]{:S(2)}) copy-start(bf16[256,1024]{1,0:T(8,128)(2,1)} %get-tuple-element.16) | copy-start | bytes 1572868
  56.4 99.4 %copy-start.1 = (bf16[256,1024]{1,0:T(8,128)(2,1)S(1)}, bf16[256,1024]{1,0:T(8,128)(2,1)}, u32[]{:S(2)}) copy-start(bf16[256,1024]{1,0:T(8,128)(2,1)} %get-tuple-element.17) | copy-start | bytes 1572868
  56.4 100.2 %copy-start = (bf16[256,1024]{1,0:T(8,128)(2,1)S(1)}, bf16[256,1024]{1,0:T(8,128)(2,1)}, u32[]{:S(2)}) copy-start(bf16[256,1024]{1,0:T(8,128)(2,1)} %get-tuple-element.18) | copy-start | bytes 1572868
Sparse Core Ops, SparseCore 0:
  56.6 98.3 reduce-scatter.1

commit v2 on v1

--- a/solution.py
+++ b/solution.py
@@ -26,7 +26,7 @@
 def kernel(
     n, chunks, k_hbm, v_hbm, q_ref, w_ref, go_ref, bias_ref,
     dq_ref, dk_ref, dv_ref, wg_ref,
-    kv, kt, vt, s_scr, own_sem, send_sem, recv_sem,
+    kv, kt, vt, s_scr, own_sem, send_sem, recv_sem, *rs,
 ):
     rows = q_ref.shape[0]
     head_dim = PAIR // 2
@@ -83,16 +83,25 @@
     barrier = pltpu.get_barrier_semaphore()
     for neighbour in (yp, cp):
         pl.semaphore_signal(barrier, inc=1, device_id=(gid, neighbour), device_id_type=MESH)
-
-    @pl.when(has_up)
-    def _():
-        pl.semaphore_signal(barrier, inc=1, device_id=(gid, up), device_id_type=MESH)
-
-    @pl.when(has1)
-    def _():
-        pl.semaphore_signal(barrier, inc=1, device_id=(gid, down), device_id_type=MESH)
-
-    pl.semaphore_wait(barrier, 2 + (2 * nz - 2 - z) // nz + (z + nz - 1) // nz)
+    if rs:
+        for other in range(nz):
+            @pl.when(z != other)
+            def _():
+                pl.semaphore_signal(
+                    barrier, inc=1, device_id=(gid, PLANE * other + i), device_id_type=MESH
+                )
+
+        pl.semaphore_wait(barrier, 1 + nz)
+    else:
+        @pl.when(has_up)
+        def _():
+            pl.semaphore_signal(barrier, inc=1, device_id=(gid, up), device_id_type=MESH)
+
+        @pl.when(has1)
+        def _():
+            pl.semaphore_signal(barrier, inc=1, device_id=(gid, down), device_id_type=MESH)
+
+        pl.semaphore_wait(barrier, 2 + (2 * nz - 2 - z) // nz + (z + nz - 1) // nz)
 
     relay_z = jnp.logical_and(has1, has_up)
     y1, y0 = y == 1, y == 0
@@ -198,6 +207,89 @@
         @pl.when(jnp.logical_or(y1, has2))
         def _():
             done(7)
+
+    if rs:
+        heads, mine, src0, dst0, src1, dst1, src2, dst2, rs_send, rs_recv, z_recv = rs
+
+    def core_copy(ch):
+        return pltpu.make_async_remote_copy(
+            src_ref=src0.at[ch], dst_ref=dst0.at[ch],
+            send_sem=rs_send.at[0, ch], recv_sem=rs_recv.at[0, ch],
+            device_id=(gid, cp), device_id_type=MESH,
+        )
+
+    def y_copy(ch):
+        return pltpu.make_async_remote_copy(
+            src_ref=src1.at[ch], dst_ref=dst1.at[ch],
+            send_sem=rs_send.at[1, ch], recv_sem=rs_recv.at[1, ch],
+            device_id=(gid, yp), device_id_type=MESH,
+        )
+
+    def z_copy(ch, slot):
+        return pltpu.make_async_remote_copy(
+            src_ref=src2.at[ch], dst_ref=dst2.at[slot],
+            send_sem=rs_send.at[2, ch], recv_sem=z_recv.at[slot],
+            device_id=(gid, PLANE * (ch // 2) + i), device_id_type=MESH,
+        )
+
+    def reduce_core(ch, go):
+        mine[ch] = dot(heads[c], go)
+        src0[ch] = dot(heads[1 - c], go).astype(BF16)
+        core_copy(ch).start()
+
+    def reduce_y(ch):
+        core_copy(ch).wait_recv()
+        part = mine[ch] + dst0[ch].astype(F32)
+
+        @pl.when(y != lax.rem(ch, 2))
+        def _():
+            src1[ch] = part.astype(BF16)
+            y_copy(ch).start()
+
+        @pl.when(y == lax.rem(ch, 2))
+        def _():
+            mine[ch] = part
+
+    def reduce_z(ch):
+        @pl.when(y == lax.rem(ch, 2))
+        def _():
+            y_copy(ch).wait_recv()
+            part = mine[ch] + dst1[ch].astype(F32)
+
+            @pl.when(z != ch // 2)
+            def _():
+                src2[ch] = part.astype(BF16)
+                z_copy(ch, z).start()
+
+            @pl.when(z == ch // 2)
+            def _():
+                wg_ref[...] = part
+
+    def reduce_end():
+        for other in range(nz):
+            @pl.when(z != other)
+            def _():
+                pltpu.make_async_remote_copy(
+                    src_ref=src2.at[0], dst_ref=dst2.at[other],
+                    send_sem=rs_send.at[2, 0], recv_sem=z_recv.at[other],
+                    device_id=(gid, yp), device_id_type=MESH,
+                ).wait_recv()
+                wg_ref[...] += dst2[other].astype(F32)
+
+    def reduce_sent(ch):
+        core_copy(ch).wait_send()
+
+        @pl.when(y != lax.rem(ch, 2))
+        def _():
+            y_copy(ch).wait_send()
+
+        @pl.when(jnp.logical_and(y == lax.rem(ch, 2), z != ch // 2))
+        def _():
+            pltpu.make_async_remote_copy(
+                src_ref=src2.at[ch], dst_ref=dst2.at[z],
+                send_sem=rs_send.at[2, ch], recv_sem=z_recv.at[z],
+                device_id=(gid, yp), device_id_type=MESH,
+            ).wait_send()
 
     def compute(ch):
         cols = pl.ds(pl.multiple_of(ch * PAIR, PAIR), PAIR)
@@ -216,15 +308,11 @@
         for b in range(SLOTS):
             kt[b] = kv[ch, b, 0].T
             vt[b] = kv[ch, b, 1].T
-        dk = jnp.zeros((rows, PAIR), F32)
-        dv = jnp.zeros((rows, PAIR), F32)
-        attn_parts = []
-        dq_parts = []
         zero = jnp.zeros((), BF16)
+        stats = []
         for h in range(2):
             span = pl.ds(h * head_dim, head_dim)
             q_th = jnp.where(head_row == h, q_t, zero)
-            g_th = jnp.where(head_row == h, g_t, zero)
             top = None
             for b in range(SLOTS):
                 s = dot(kv[ch, b, 0], q_th)
@@ -238,14 +326,14 @@
                         ],
                         axis=0,
                     )
-                s_scr[b] = s
+                s_scr[h, b] = s
                 peak = jnp.max(s, axis=0, keepdims=True)
                 top = peak if top is None else jnp.maximum(top, peak)
             total = jnp.zeros((1, rows), F32)
             attn = jnp.zeros((head_dim, rows), F32)
             for b in range(SLOTS):
-                e = jnp.exp(s_scr[b] - top)
-                s_scr[b] = e
+                e = jnp.exp(s_scr[h, b] - top)
+                s_scr[h, b] = e
                 total = total + jnp.sum(e, axis=0, keepdims=True)
                 attn = attn + dot(vt[b, span, :], e.astype(BF16))
             inv = 1.0 / total
@@ -255,9 +343,23 @@
                 axis=0,
                 keepdims=True,
             )
+            stats.append((inv, delta, attn_low))
+            if rs:
+                heads[h] = attn_low
+        if rs:
+            reduce_core(ch, go)
+        else:
+            wg_ref[cols, :] = dot(jnp.concatenate([s[2] for s in stats], axis=0), go)
+        dk = jnp.zeros((rows, PAIR), F32)
+        dv = jnp.zeros((rows, PAIR), F32)
+        dq_parts = []
+        for h in range(2):
+            span = pl.ds(h * head_dim, head_dim)
+            inv, delta, _ = stats[h]
+            g_th = jnp.where(head_row == h, g_t, zero)
             dq = jnp.zeros((head_dim, rows), F32)
             for b in range(SLOTS):
-                e = s_scr[b]
+                e = s_scr[h, b]
                 ds = e * (dot(kv[ch, b, 1], g_th) - delta)
                 dq = dq + dot(kt[b, span, :], ds.astype(BF16))
                 if b == OWN:
@@ -265,12 +367,10 @@
                         (ds * inv).astype(BF16), jnp.where(head_col == h, qs, zero)
                     )
                     dv = dv + dot((e * inv).astype(BF16), jnp.where(head_col == h, g, zero))
-            attn_parts.append(attn_low)
             dq_parts.append(dq * (inv * scale))
         dq_ref[:, cols] = jnp.concatenate(dq_parts, axis=0).T.astype(BF16)
         dk_ref[:, cols] = dk.astype(BF16)
         dv_ref[:, cols] = dv.astype(BF16)
-        wg_ref[cols, :] = dot(jnp.concatenate(attn_parts, axis=0), go)
 
     def step(t, carry):
         for lag, stage in enumerate((stage0, stage1, stage2, stage3)):
@@ -281,14 +381,27 @@
         @pl.when(t >= 4)
         def _():
             stage4(t - 4)
+            if rs:
+                @pl.when(t >= 5)
+                def _():
+                    reduce_z(t - 5)
+
             compute(t - 4)
+            if rs:
+                reduce_y(t - 4)
 
         return carry
 
     lax.fori_loop(0, chunks + 4, step, 0)
+
+    if rs:
+        reduce_z(chunks - 1)
+        reduce_end()
 
     def finish(ch, carry):
         sent(ch)
+        if rs:
+            reduce_sent(ch)
         return carry
 
     lax.fori_loop(0, chunks, finish, 0)
@@ -312,28 +425,42 @@
     chunks = width // PAIR
     sid = lax.axis_index("span")
     bias = block_bias(track, sid, rows)
+    share = width // n
+    inside = 2 * share == PAIR and n % PLANE == 0
     grad = jax.ShapeDtypeStruct((rows, width), BF16)
+    wg_rows = share if inside else width
+    term = (share, width)
+    rs = [
+        pltpu.VMEM((2, share, rows), BF16),
+        pltpu.VMEM((chunks, *term), F32),
+        *[pltpu.VMEM((chunks, *term), BF16)] * 5,
+        pltpu.VMEM((n // PLANE, *term), BF16),
+        pltpu.SemaphoreType.DMA((3, chunks)),
+        pltpu.SemaphoreType.DMA((2, chunks)),
+        pltpu.SemaphoreType.DMA((n // PLANE,)),
+    ]
     vmem = pl.BlockSpec(memory_space=pltpu.VMEM)
     dq, dk, dv, wg = pl.pallas_call(
         functools.partial(kernel, n, chunks),
-        out_shape=(grad, grad, grad, jax.ShapeDtypeStruct((width, width), F32)),
+        out_shape=(grad, grad, grad, jax.ShapeDtypeStruct((wg_rows, width), F32)),
         in_specs=[pl.BlockSpec(memory_space=pl.ANY)] * 2 + [vmem] * 4,
         out_specs=(vmem,) * 4,
         scratch_shapes=[
             pltpu.VMEM((chunks, SLOTS, 2, rows, PAIR), BF16),
             pltpu.VMEM((SLOTS, PAIR, rows), BF16),
             pltpu.VMEM((SLOTS, PAIR, rows), BF16),
-            pltpu.VMEM((SLOTS, rows, rows), F32),
+            pltpu.VMEM((2, SLOTS, rows, rows), F32),
             pltpu.SemaphoreType.DMA((chunks, 2)),
             pltpu.SemaphoreType.DMA((8, chunks)),
             pltpu.SemaphoreType.DMA((chunks, OWN)),
-        ],
+        ] + (rs if inside else []),
         compiler_params=pltpu.CompilerParams(
             collective_id=0, has_side_effects=True, vmem_limit_bytes=60 * 1024 * 1024
         ),
     )(keys, values, queries, out_weight, grad_out, bias)
-    weight_grad = lax.psum_scatter(wg, "span", scatter_dimension=0, tiled=True)
-    return (dq, dk, dv, weight_grad)
+    if not inside:
+        wg = lax.psum_scatter(wg, "span", scatter_dimension=0, tiled=True)
+    return (dq, dk, dv, wg)
 
 
 def solution(mesh):

time: 164 us -> 119 us (0.73)
  the two profiles are of different devices: /device:TPU:0 before, /device:TPU:28 now
where the time goes in v2:
time: 119 us; the launch traced here: 118 us
  Pallas kernels  111 us (93%)
  local copies, waits for them, and re-layouts  6.1 us (5%)
    pallas_call x1, Pallas kernels, shards(): pl.pallas_call(functools.partial(kernel, n, chunks), out_shape=(grad, gra...  111 us
    unnamed x9, local copies, waits for them, and re-layouts  5.93 us

profile of v2, /device:TPU:28, one launch (start us, length us, event | category | flops | bytes accessed | tf_op | source)
XLA Modules:
  0.0 118.4 jit_solution(4665947468391214303)
XLA Ops:
  0.7 0.1 iota_compare_fusion
  0.7 0.8 select_reduce_fusion
  1.5 0.1 copy.10
  1.6 0.1 broadcast_in_dim.41
  1.7 0.6 copy.13
  2.3 110.7 %shard_map.93 = (bf16[256,1024]{1,0:T(8,128)(2,1)}, bf16[256,1024]{1,0:T(8,128)(2,1)}, bf16[256,1024]{1,0:T(8,128)(2,1)}, f32[64,1024]{1,0:T(8,128)}) custom-call(bf16[256,1024]{1,0:T(8,128)(2,1)} %k_hbm.1, bf16[256,1024]{1,0:T(8,128)(2,1)} %v_hbm.1, bf16[256,1024]{1,0:T(8,128)(2,1)} %q_ref.1, bf16[1024,1024]{1,0:T(8,128)(2,1)} %w_ref.1, ...), custom_call_target="tpu_custom_call" | custom-call | tf_op jit(solution)/shard_map/pallas_call | solution.py:443
  113.1 0.0 copy-start
  113.1 0.0 copy-start.1
  113.1 1.9 %copy.18 = bf16[256,1024]{1,0:T(8,128)(2,1)} copy(bf16[256,1024]{1,0:T(8,128)(2,1)} %get-tuple-element.8) | data formatting | bytes 1048576
  115.0 1.9 %copy.19 = bf16[256,1024]{1,0:T(8,128)(2,1)} copy(bf16[256,1024]{1,0:T(8,128)(2,1)} %get-tuple-element.9) | data formatting | bytes 1048576
  116.9 0.0 copy-done
  116.9 0.8 copy.20
  117.7 0.0 copy-done.1
  117.7 0.7 copy.21
  (3 shorter events, 0.0 us)
Async XLA Ops:
  113.1 3.8 %copy-start = (bf16[256,1024]{1,0:T(8,128)(2,1)S(1)}, bf16[256,1024]{1,0:T(8,128)(2,1)}, u32[]{:S(2)}) copy-start(bf16[256,1024]{1,0:T(8,128)(2,1)} %get-tuple-element.10) | copy-start | bytes 1572868
  113.1 4.6 %copy-start.1 = (f32[64,1024]{1,0:T(8,128)S(1)}, f32[64,1024]{1,0:T(8,128)}, u32[]{:S(2)}) copy-start(f32[64,1024]{1,0:T(8,128)} %get-tuple-element.11) | copy-start | bytes 786436

commit v3 on v2

--- a/solution.py
+++ b/solution.py
@@ -381,20 +381,27 @@
         @pl.when(t >= 4)
         def _():
             stage4(t - 4)
-            if rs:
-                @pl.when(t >= 5)
+            compute(t - 4)
+
+        if rs:
+            for k, (ys, zs) in enumerate(((3, 0), (5, 3), (6, 5), (7, 6))):
+                y_from = (0, 3, 5, 6)[k]
+                z_from = (0, 0, 3, 5)[k]
+
+                @pl.when(t == chunks + k)
                 def _():
-                    reduce_z(t - 5)
-
-            compute(t - 4)
-            if rs:
-                reduce_y(t - 4)
+                    for ch in range(y_from, ys):
+                        reduce_y(ch)
+                    for ch in range(z_from, zs):
+                        reduce_z(ch)
 
         return carry
 
     lax.fori_loop(0, chunks + 4, step, 0)
 
     if rs:
+        reduce_y(chunks - 1)
+        reduce_z(chunks - 2)
         reduce_z(chunks - 1)
         reduce_end()
 
@@ -455,7 +462,7 @@
             pltpu.SemaphoreType.DMA((chunks, OWN)),
         ] + (rs if inside else []),
         compiler_params=pltpu.CompilerParams(
-            collective_id=0, has_side_effects=True, vmem_limit_bytes=60 * 1024 * 1024
+            collective_id=0, has_side_effects=True, vmem_limit_bytes=36 * 1024 * 1024
         ),
     )(keys, values, queries, out_weight, grad_out, bias)
     if not inside:

time: 119 us -> 91.6 us (0.77)
  Pallas kernels: 111 us -> 80.6 us
  local copies, waits for them, and re-layouts: 6.1 us -> 9.01 us
    pallas_call x1, Pallas kernels: 111 us -> 80.6 us  [shards(): pl.pallas_call(functools.partial(kernel, n, chunks), out_shape=(grad, gra...]
    unnamed x9 -> x15, local copies, waits for them, and re-layouts: 5.93 us -> 8.84 us
where the time goes in v3:
time: 91.6 us; the launch traced here: 91.2 us
  Pallas kernels  80.6 us (88%)
  local copies, waits for them, and re-layouts  9.01 us (10%)
    pallas_call x1, Pallas kernels, shards(): pl.pallas_call(functools.partial(kernel, n, chunks), out_shape=(grad, gra...  80.6 us
    unnamed x15, local copies, waits for them, and re-layouts  8.84 us

profile of v3, /device:TPU:28, one launch (start us, length us, event | category | flops | bytes accessed | tf_op | source)
XLA Modules:
  0.0 91.2 jit_solution(17195182778247991684)
XLA Ops:
  0.7 0.1 iota_compare_fusion
  0.7 0.8 select_reduce_fusion
  1.5 0.1 copy.10
  1.6 0.1 broadcast_in_dim.41
  1.7 0.0 copy-start
  1.7 1.6 %copy-done = bf16[1024,1024]{1,0:T(8,128)(2,1)S(1)} copy-done((bf16[1024,1024]{1,0:T(8,128)(2,1)S(1)}, bf16[1024,1024]{1,0:T(8,128)(2,1)}, u32[]{:S(2)}) %copy-start) | copy-done | bytes 2097176
  3.3 0.0 copy-start.1
  3.3 1.0 %copy-done.1 = bf16[256,1024]{1,0:T(8,128)(2,1)S(1)} copy-done((bf16[256,1024]{1,0:T(8,128)(2,1)S(1)}, bf16[256,1024]{1,0:T(8,128)(2,1)}, u32[]{:S(2)}) %copy-start.1) | copy-done | bytes 524312
  4.4 0.0 copy-start.2
  4.4 1.0 %copy-done.2 = bf16[256,1024]{1,0:T(8,128)(2,1)S(1)} copy-done((bf16[256,1024]{1,0:T(8,128)(2,1)S(1)}, bf16[256,1024]{1,0:T(8,128)(2,1)}, u32[]{:S(2)}) %copy-start.2) | copy-done | bytes 524312
  5.4 0.0 copy-start.3
  5.4 1.0 %copy-done.3 = bf16[256,1024]{1,0:T(8,128)(2,1)S(1)} copy-done((bf16[256,1024]{1,0:T(8,128)(2,1)S(1)}, bf16[256,1024]{1,0:T(8,128)(2,1)}, u32[]{:S(2)}) %copy-start.3) | copy-done | bytes 524312
  6.4 0.0 copy-start.4
  6.4 1.0 %copy-done.4 = bf16[256,1024]{1,0:T(8,128)(2,1)S(1)} copy-done((bf16[256,1024]{1,0:T(8,128)(2,1)S(1)}, bf16[256,1024]{1,0:T(8,128)(2,1)}, u32[]{:S(2)}) %copy-start.4) | copy-done | bytes 524312
  7.5 80.6 %shard_map.93 = (bf16[256,1024]{1,0:T(8,128)(2,1)S(1)}, bf16[256,1024]{1,0:T(8,128)(2,1)S(1)}, bf16[256,1024]{1,0:T(8,128)(2,1)S(1)}, f32[64,1024]{1,0:T(8,128)S(1)}) custom-call(bf16[256,1024]{1,0:T(8,128)(2,1)S(1)} %copy-done.1, bf16[256,1024]{1,0:T(8,128)(2,1)S(1)} %copy-done.2, bf16[256,1024]{1,0:T(8,128)(2,1)S(1)} %copy-done.3, ...), custom_call_target="tpu_custom_call" | custom-call | tf_op jit(solution)/shard_map/pallas_call | solution.py:450
  88.1 0.8 copy.18
  88.9 0.8 copy.19
  89.7 0.8 copy.20
  90.5 0.7 copy.21
  (4 shorter events, 0.0 us)
Async XLA Ops:
  1.7 1.6 %copy-start = (bf16[1024,1024]{1,0:T(8,128)(2,1)S(1)}, bf16[1024,1024]{1,0:T(8,128)(2,1)}, u32[]{:S(2)}) copy-start(bf16[1024,1024]{1,0:T(8,128)(2,1)} %w_ref.1) | copy-start | bytes 6291460
  3.3 1.0 %copy-start.1 = (bf16[256,1024]{1,0:T(8,128)(2,1)S(1)}, bf16[256,1024]{1,0:T(8,128)(2,1)}, u32[]{:S(2)}) copy-start(bf16[256,1024]{1,0:T(8,128)(2,1)} %k_hbm.1) | copy-start | bytes 1572868
  4.4 1.0 %copy-start.2 = (bf16[256,1024]{1,0:T(8,128)(2,1)S(1)}, bf16[256,1024]{1,0:T(8,128)(2,1)}, u32[]{:S(2)}) copy-start(bf16[256,1024]{1,0:T(8,128)(2,1)} %v_hbm.1) | copy-start | bytes 1572868
  5.4 1.0 %copy-start.3 = (bf16[256,1024]{1,0:T(8,128)(2,1)S(1)}, bf16[256,1024]{1,0:T(8,128)(2,1)}, u32[]{:S(2)}) copy-start(bf16[256,1024]{1,0:T(8,128)(2,1)} %q_ref.1) | copy-start | bytes 1572868
  6.4 1.0 %copy-start.4 = (bf16[256,1024]{1,0:T(8,128)(2,1)S(1)}, bf16[256,1024]{1,0:T(8,128)(2,1)}, u32[]{:S(2)}) copy-start(bf16[256,1024]{1,0:T(8,128)(2,1)} %go_ref.1) | copy-start | bytes 1572868
